TPU v7x, 128 devices: a whole 4x4x4 slice. The times are simulated.
128 devices in a mesh: batch: 8 (over z, x_lo), rows: 8 (over x_hi, y), section: 2 (over core).
Axes of the slice: x: 4 (x_hi: 2, x_lo: 2; x = x_hi * 2 + x_lo), y: 4, z: 4, core: 2. Of those that a mesh axis runs over, the one named last changes fastest.
Arguments:
- features: bfloat16 [32, 32, 32, 1536], P('batch', 'rows'), may hold values from -6 to 6, as said below
- dw_kernel: bfloat16 [7, 7, 1536], replicated, may hold values from -0.875 to 0.875
- ln_gain: bfloat16 [1536], replicated, may hold values from 0.25 to 1.75
- widening_pointwise_matrix: bfloat16 [1536, 3072], P(None, 'section'), may hold values from -0.15625 to 0.15625
- w_reduce: bfloat16 [3072, 1536], P('section'), may hold values from -0.109375 to 0.109375
- layer_branch_scale: bfloat16 [1536], replicated, may hold values from 0.5 to 2
- p_expand: bfloat16 [1536, 2048], P(None, 'section'), may hold values from -0.15625 to 0.15625
- p_kernel: bfloat16 [9, 2048, 256], P(None, 'section'), may hold values from -0.046875 to 0.046875
- region_ids: int32 [32, 32, 32], P('batch', 'rows'), may hold values from 0 to 63, as said below
- owner_slot: int32 [8, 256], P('batch'), may hold values from 0 to 255, each once within a row
- partner: int32 [32, 64], P('batch'), may hold values from 0 to 63
- key_embed: bfloat16 [2048, 256], P(('batch', 'rows')), may hold values from -6 to 6
Outputs:
- region_embed: float32 [2048, 256], P(('batch', 'rows'))
- region_loss: float32 [2048], P(('batch', 'rows'))
Inputs may be any that keep to these rules, and one draw needn't show every extreme that they name: `features`: exactly one image other than image 0 has all its entries zero. `region_ids`: each image uses regions 0 to K - 1 for its own K of at least 16, every one of them on some pixel; image 0 uses all 64. `owner_slot`: each row is a permutation of the slots of one batch index.
All inputs are finite; a program needn't handle non-finite values.
Results may differ from a plain program's by a relative error of at most 0.0024.
Values may be sent and summed in bfloat16 or wider, within the bound.
A program may use at most 128 MiB of HBM per device.

v0:
```python
import jax
import jax.numpy as jnp
from jax import lax
from jax.sharding import PartitionSpec as P

REG = 64


sharpness_divisor = 0.1
ln_eps = 1e-06
norm_eps = 1e-06


def laid_out(blocks, dim):
    blocks = jnp.moveaxis(blocks, 0, dim)
    lengths = blocks.shape
    return blocks.reshape(*lengths[:dim], lengths[dim] * lengths[dim + 1], *lengths[dim + 2 :])


def from_everyone(shard, axis):
    copies = jnp.broadcast_to(shard, (lax.axis_size(axis), *shard.shape))
    return lax.all_to_all(copies, axis, split_axis=0, concat_axis=0, tiled=True)


def gather_directly(shard, axis, dim):
    return laid_out(from_everyone(shard, axis), dim)


def padded_2(shard, sides, width):
    for axis, dim in sides:
        size, length = (lax.axis_size(axis), shard.shape[dim])
        up = [(i, (i + 1) % size) for i in range(size - 1)]
        down = [(j, i) for i, j in up]
        last = lax.slice_in_dim(shard, length - width, length, axis=dim)
        initial = lax.slice_in_dim(shard, 0, width, axis=dim)
        before = lax.ppermute(last, axis, up)
        after = lax.ppermute(initial, axis, down)
        shard = jnp.concatenate([before, shard, after], axis=dim)
    return shard


def over_copies(shard, axis):
    everything = from_everyone(shard, axis)
    return jnp.sum(everything, axis=0)


def in_blocks(shard, dim, length):
    lengths = shard.shape
    blocks = shard.reshape(*lengths[:dim], length, lengths[dim] // length, *lengths[dim + 1 :])
    return jnp.moveaxis(blocks, dim, 0)


def sent_and_summed(shard, axis, dim):
    length = lax.axis_size(axis)
    blocks = lax.all_to_all(in_blocks(shard, dim, length), axis, 0, 0, tiled=True)
    return jnp.sum(blocks, axis=0)


def body(
    features,
    dw_kernel,
    ln_gain,
    widening_pointwise_matrix,
    w_reduce,
    layer_branch_scale,
    p_expand,
    p_kernel,
    region_ids,
    owner_slot,
    partner,
    key_embed,
):
    images, row_count, col_count, channels = features.shape
    keys_all = gather_directly(key_embed, ("batch", "rows"), 0)
    padded = padded_2(features, (("rows", 1),), 3)
    taps = lax.conv_general_dilated(
        padded,
        dw_kernel.reshape(7, 7, 1, channels),
        (1, 1),
        ((0, 0), (3, 3)),
        dimension_numbers=("NHWC", "HWIO", "NHWC"),
        feature_group_count=channels,
        preferred_element_type=jnp.float32,
    )
    average = jnp.mean(taps, axis=-1, keepdims=True)
    spread = jnp.mean(jnp.square(taps - average), axis=-1, keepdims=True)
    normed = ((taps - average) * lax.rsqrt(spread + ln_eps) * ln_gain.astype(jnp.float32)).astype(
        jnp.bfloat16
    )
    inner_act = jax.nn.gelu(
        jnp.dot(
            normed.reshape(-1, channels),
            widening_pointwise_matrix,
            preferred_element_type=jnp.float32,
        ),
        approximate=False,
    ).astype(jnp.bfloat16)
    branch = jnp.dot(inner_act, w_reduce, preferred_element_type=jnp.float32).reshape(
        images, row_count, col_count, channels
    )
    scale_vec = layer_branch_scale.astype(jnp.float32)
    segment_aggregate = over_copies(branch, "section")
    block_out = (features.astype(jnp.float32) + scale_vec * segment_aggregate).astype(jnp.bfloat16)
    in_shape = block_out.shape
    product = jnp.dot(block_out.reshape(-1, channels), p_expand, preferred_element_type=jnp.float32)
    hidden = (
        jnp.maximum(product, 0.0)
        .astype(jnp.bfloat16)
        .reshape(in_shape[0], in_shape[1], in_shape[2], p_expand.shape[1])
    )
    hidden_extended = padded_2(hidden, (("rows", 1),), 1)
    hidden_local = p_expand.shape[1]
    partial_value = lax.conv_general_dilated(
        hidden_extended,
        p_kernel.reshape(3, 3, hidden_local, p_kernel.shape[2]),
        (1, 1),
        ((0, 0), (1, 1)),
        dimension_numbers=("NHWC", "HWIO", "NHWC"),
        preferred_element_type=jnp.float32,
    )
    out_dim = partial_value.shape[-1]
    pixel_total = row_count * col_count
    region_table = jnp.arange(REG, dtype=jnp.int32)
    onehot = (region_ids.reshape(images, 1, pixel_total) == region_table[None, :, None]).astype(
        jnp.float32
    )
    counts = jnp.sum(onehot, axis=2).reshape(images * REG)
    slot_count = images * REG
    slot_iota = jnp.arange(slot_count, dtype=jnp.int32)
    inverse = jnp.zeros((slot_count,), jnp.int32).at[owner_slot[0]].set(slot_iota)
    keys_float = keys_all.astype(jnp.float32)
    unit_length_anchors = keys_float * lax.rsqrt(
        jnp.sum(keys_float * keys_float, axis=1, keepdims=True) + norm_eps
    )
    proj_sum = over_copies(partial_value, "section")
    pooled = jnp.einsum(
        "grp,gpo->gro",
        onehot,
        proj_sum.reshape(images, pixel_total, out_dim),
        precision=lax.Precision.HIGHEST,
    )
    ordered = pooled.reshape(slot_count, out_dim)[inverse]
    owned, owned_region_counts = (
        sent_and_summed(ordered, "rows", 0),
        sent_and_summed(counts[inverse], "rows", 0),
    )
    per_owner = slot_count // lax.axis_size("rows")
    pos_count = owned.shape[0]
    slot_list = lax.dynamic_slice_in_dim(inverse, lax.axis_index("rows") * per_owner, pos_count, 0)
    image_local = slot_list // REG
    region = slot_list % REG
    global_image = lax.axis_index("batch") * images + image_local
    positive = global_image * REG + partner[image_local, region]
    probe_vectors = owned * lax.rsqrt(jnp.sum(owned * owned, axis=1, keepdims=True) + norm_eps)
    cosine_match_matrix = (
        jnp.einsum("tq,bq->tb", probe_vectors, unit_length_anchors, precision=lax.Precision.HIGHEST)
        / sharpness_divisor
    )
    log_total = jnp.log(jnp.sum(jnp.exp(cosine_match_matrix), axis=1))
    pos_logit = jnp.take_along_axis(cosine_match_matrix, positive[:, None], axis=1)[:, 0]
    probe_vectors, region_loss = (
        probe_vectors,
        jnp.where(owned_region_counts > 0.5, log_total - pos_logit, 0.0),
    )
    return (probe_vectors, region_loss)


def solution(mesh):
    in_specs = (
        P("batch", "rows", None, None),
        P(),
        P(),
        P(None, "section"),
        P("section", None),
        P(),
        P(None, "section"),
        P(None, "section", None),
        P("batch", "rows", None),
        P("batch", None),
        P("batch", None),
        P(("batch", "rows"), None),
    )
    out_specs = (P(("batch", "rows"), None), P(("batch", "rows")))
    return jax.shard_map(body, mesh=mesh, in_specs=in_specs, out_specs=out_specs, check_vma=False)
```

profile of v0, /device:TPU:1, one launch (start us, length us, event | category | flops | bytes accessed | tf_op | source)
XLA Modules:
  0.0 177.9 jit_solution(1542148767497596384)
XLA Ops:
  0.6 2.8 %copy.43 = bf16[4,4,32,1536]{3,0,2,1:T(4,128)(2,1)S(1)} copy(bf16[4,4,32,1536]{3,2,1,0:T(8,128)(2,1)} %param.12) | data formatting | bytes 3145728 | tf_op args[0]
  3.4 1.1 copy-done.2
  4.6 2.1 %fusion.98 = (bf16[4,3,32,1536]{3,0,2,1:T(4,128)(2,1)}, bf16[4,3,32,1536]{3,0,2,1:T(4,128)(2,1)}) fusion(bf16[4,4,32,1536]{3,0,2,1:T(4,128)(2,1)S(1)} %copy.43), kind=kLoop, calls=%fused_computation.143 | loop fusion | bytes 4718592 | tf_op jit(solution)/shard_map/slice | solution.py:34
  6.7 5.1 %collective-permute-start = (bf16[4,3,32,1536]{3,0,2,1:T(4,128)(2,1)}, bf16[4,3,32,1536]{3,0,2,1:T(4,128)(2,1)}, u32[]{:S(2)}, u32[]{:S(2)}) collective-permute-start(bf16[4,3,32,1536]{3,0,2,1:T(4,128)(2,1)} %get-tuple-element.4), channel_id=1, source_target_pairs={{0,2},{2,4},{4,6},{6,8},{8,10},{10,12},{12,14},{1,3},{3,5},{5,7},{... | collective-permute-start | bytes 3538952 | tf_op jit(solution)/shard_map/ppermute | solution.py:36
  11.8 1.3 collective-permute-start.1
  13.4 1.4 scatter_custom_fusion
  14.8 1.9 %gather_fusion.1 = f32[256]{0:T(256)S(1)} fusion(f32[256]{0:T(256)S(1)} %reshape.135, s32[1024]{0:T(1024)S(1)} %pad_clamp_fusion), kind=kCustom, calls=%fused_computation.1 | custom fusion | bytes 3072 | tf_op jit(solution)/shard_map/gather | solution.py:145
  16.7 0.7 all_to_all.21
  17.4 7.4 %all-to-all-start.3 = ((f32[8,1,32]{2,1,0:T(1,128)}), f32[8,1,32]{2,1,0:T(1,128)S(1)}, u32[]{:S(2)}, u32[]{:S(2)}) async-start(f32[8,1,32]{2,1,0:T(1,128)} %all_to_all.21), calls=%async_computation.3 | async-start | bytes 8192 | tf_op jit(solution)/shard_map/all_to_all | solution.py:55
  24.9 0.8 gather_fusion.2
  25.7 18.5 %all-to-all-done.3 = f32[8,1,32]{2,1,0:T(1,128)S(1)} async-done(((f32[8,1,32]{2,1,0:T(1,128)}), f32[8,1,32]{2,1,0:T(1,128)S(1)}, u32[]{:S(2)}, u32[]{:S(2)}) %all-to-all-start.3) | async-done | bytes 1056 | tf_op jit(solution)/shard_map/all_to_all | solution.py:55
  44.3 19.8 %fusion.100 = (f32[4,4,32]{0,2,1:T(8,128)S(1)}, f32[4,4,32,1536]{3,0,2,1:T(4,128)S(1)}) fusion(bf16[7,7,1,1536]{3,1,0,2:T(8,128)(2,1)S(1)} %bitcast.54, bf16[4,3,32,1536]{3,0,2,1:T(4,128)(2,1)} %collective-permute-done.1, bf16[4,4,32,1536]{3,0,2,1:T(4,128)(2,1)} %copy-done.2, bf16[4,3,32,1536]{3,0,2,1:T(4,128)(2,1)} %collective-permute-done), kind=kOutput, calls=%fused_computation.145 | convolution fusion | flops 85523968 | bytes 7230464 | tf_op jit(solution)/shard_map/conv_general_dilated | solution.py:76
  64.1 1.0 multiply_reduce_fusion
  65.0 1.0 multiply_convert_fusion
  66.0 1.4 copy.47
  67.5 15.9 %fusion.21 = f32[512,1536]{1,0:T(8,128)} fusion(bf16[1536,1536]{1,0:T(8,128)(2,1)} %param.16, bf16[512,1536]{1,0:T(8,128)(2,1)} %bitcast.46, bf16[1536,1536]{1,0:T(8,128)(2,1)} %param.15), kind=kOutput, calls=%fused_computation.43 | convolution fusion | flops 4882956288 | bytes 14155776 | tf_op jit(solution)/shard_map/dot_general | solution.py:98
  83.4 2.7 %broadcast_in_dim.36 = f32[2,4,4,32,1536]{4,3,2,1,0:T(8,128)S(1)} broadcast(f32[4,4,32,1536]{3,2,1,0:T(8,128)} %bitcast.43), dimensions={1,2,3,4} | broadcast | bytes 9437184 | tf_op jit(solution)/shard_map/broadcast_in_dim | solution.py:21
  86.1 11.7 %all_to_all.29 = f32[2,4,4,32,1536]{4,3,2,1,0:T(8,128)} all-to-all(f32[2,4,4,32,1536]{4,3,2,1,0:T(8,128)S(1)} %broadcast_in_dim.36), channel_id=1, replica_groups=mesh['batch'=8,'rows'=8,'section'=2] {'section'}, dimensions={0} | all-to-all | bytes 12582912 | tf_op jit(solution)/shard_map/all_to_all | solution.py:22
  97.8 1.1 broadcast_in_dim.39
  98.9 8.9 %all-to-all-start.4 = ((bf16[64,32,256]{2,1,0:T(8,128)(2,1)}), bf16[64,32,256]{2,1,0:T(8,128)(2,1)}, u32[]{:S(2)}, u32[]{:S(2)}) async-start(bf16[64,32,256]{2,1,0:T(8,128)(2,1)} %broadcast_in_dim.39), calls=%async_computation.4 | async-start | bytes 2097152 | tf_op jit(solution)/shard_map/all_to_all | solution.py:22
  107.8 5.4 %reduce_sum.92 = f32[4,4,32,1536]{3,2,1,0:T(8,128)} reduce(f32[2,4,4,32,1536]{4,3,2,1,0:T(8,128)} %all_to_all.29, f32[]{:T(128)} %constant.48.clone.1), dimensions={0}, to_apply=%region_2.0 | reduce | flops 786432 | bytes 9437188 | tf_op jit(solution)/shard_map/reduce_sum | solution.py:44
  113.3 2.8 %add_convert_fusion = bf16[4,4,32,1536]{3,2,1,0:T(8,128)(2,1)S(1)} fusion(f32[4,4,32,1536]{3,2,1,0:T(8,128)} %reduce_sum.92, bf16[4,4,32,1536]{3,2,1,0:T(8,128)(2,1)} %param.12, f32[1536]{0:T(1024)S(1)} %convert_element_type.34), kind=kLoop, calls=%fused_computation.17 | loop fusion | flops 3145728 | bytes 6297600 | tf_op jit(solution)/shard_map/convert_element_type | solution.py:103
  116.1 1.9 %maximum_convert_fusion = bf16[512,1024]{1,0:T(8,128)(2,1)S(1)} fusion(bf16[512,1536]{1,0:T(8,128)(2,1)S(1)} %bitcast.47, bf16[1536,1024]{1,0:T(8,128)(2,1)S(1)} %copy-done), kind=kOutput, calls=%fused_computation.42 | convolution fusion | flops 1611661312 | bytes 5767168 | tf_op jit(solution)/shard_map/dot_general | solution.py:105
  118.0 0.8 copy.48
  118.8 1.0 copy-done.3
  119.8 1.0 fusion.99
  120.8 2.8 %collective-permute-start.2 = (bf16[4,1,32,1024]{3,0,2,1:T(4,128)(2,1)}, bf16[4,1,32,1024]{3,0,2,1:T(4,128)(2,1)S(1)}, u32[]{:S(2)}, u32[]{:S(2)}) collective-permute-start(bf16[4,1,32,1024]{3,0,2,1:T(4,128)(2,1)} %get-tuple-element.6), channel_id=1, source_target_pairs={{0,2},{2,4},{4,6},{6,8},{8,10},{10,12},{12,14},{1,3},{3,5},{5,7},{... | collective-permute-start | bytes 786440 | tf_op jit(solution)/shard_map/ppermute | solution.py:36
  123.7 1.3 collective-permute-start.3
  125.0 0.3 all-to-all-done.4
  125.2 1.6 multiply_reduce_fusion.1
  126.9 1.8 %collective-permute-done.2 = bf16[4,1,32,1024]{3,0,2,1:T(4,128)(2,1)S(1)} collective-permute-done((bf16[4,1,32,1024]{3,0,2,1:T(4,128)(2,1)}, bf16[4,1,32,1024]{3,0,2,1:T(4,128)(2,1)S(1)}, u32[]{:S(2)}, u32[]{:S(2)}) %collective-permute-start.2) | collective-permute-done | bytes 262176 | tf_op jit(solution)/shard_map/ppermute | solution.py:36
  128.7 3.8 %collective-permute-done.3 = bf16[4,1,32,1024]{3,0,2,1:T(4,128)(2,1)} collective-permute-done((bf16[4,1,32,1024]{3,0,2,1:T(4,128)(2,1)}, bf16[4,1,32,1024]{3,0,2,1:T(4,128)(2,1)}, u32[]{:S(2)}, u32[]{:S(2)}) %collective-permute-start.3) | collective-permute-done | bytes 262176 | tf_op jit(solution)/shard_map/ppermute | solution.py:37
  132.5 2.5 %maximum_bitcast_fusion = bf16[6,4,32,1024]{3,1,2,0:T(4,128)(2,1)S(1)} fusion(bf16[4,1,32,1024]{3,0,2,1:T(4,128)(2,1)} %collective-permute-done.3, bf16[4,4,32,1024]{3,0,2,1:T(4,128)(2,1)} %copy-done.3, bf16[4,1,32,1024]{3,0,2,1:T(4,128)(2,1)S(1)} %collective-permute-done.2), kind=kLoop, calls=%fused_computation.44 | loop fusion | flops 1572864 | bytes 3145728 | tf_op jit(solution)/shard_map/concatenate | solution.py:38
  135.0 0.8 pad
  135.9 0.4 slice.30
  136.3 1.3 fusion.17
  137.6 5.6 %fusion.53 = f32[4,32,5,256]{3,1,2,0:T(8,128)S(1)} fusion(bf16[3,3,1024,256]{3,2,1,0:T(8,128)(2,1)} %bitcast.53, bf16[6,4,8,7,1024]{4,1,3,2,0:T(4,128)(2,1)S(1)} %fusion.17, pred[32,5]{0,1:T(8,128)(4,1)S(1)} %copy-done.11), kind=kOutput, calls=%fused_computation.75 | convolution fusion | flops 3020062720 | bytes 8126624 | tf_op jit(solution)/shard_map/conv_general_dilated | solution.py:113
  143.2 0.4 copy.52
  143.9 7.2 %all_to_all.30 = f32[2,4,4,32,256]{4,3,2,1,0:T(8,128)} all-to-all(f32[2,4,4,32,256]{4,3,2,1,0:T(8,128)S(1)} %broadcast_in_dim.37), channel_id=1, replica_groups=mesh['batch'=8,'rows'=8,'section'=2] {'section'}, dimensions={0} | all-to-all | bytes 2097152 | tf_op jit(solution)/shard_map/all_to_all | solution.py:22
  151.1 2.2 %reduce_sum.93 = f32[4,4,32,256]{3,2,1,0:T(8,128)} reduce(f32[2,4,4,32,256]{4,3,2,1,0:T(8,128)} %all_to_all.30, f32[]{:T(128)} %constant.48.clone.1), dimensions={0}, to_apply=%region_3.0 | reduce | flops 131072 | bytes 1572868 | tf_op jit(solution)/shard_map/reduce_sum | solution.py:44
  153.3 1.4 fusion.57
  154.6 1.7 gather_fusion
  156.3 8.8 %all-to-all-start.2 = ((f32[8,32,256]{2,1,0:T(8,128)}), f32[8,32,256]{2,1,0:T(8,128)S(1)}, u32[]{:S(2)}, u32[]{:S(2)}) async-start(f32[8,32,256]{2,1,0:T(8,128)} %bitcast.48), calls=%async_computation.2 | async-start | bytes 524288 | tf_op jit(solution)/shard_map/all_to_all | solution.py:55
  165.1 2.9 %bitcast_multiply_fusion = f32[2048,256]{1,0:T(8,128)} fusion(f32[2048]{0:T(1024)S(1)} %rsqrt.30, bf16[64,32,256]{2,1,0:T(8,128)(2,1)} %all-to-all-done.4), kind=kLoop, calls=%fused_computation.40 | loop fusion | flops 1048576 | bytes 3153920 | tf_op jit(solution)/shard_map/mul | solution.py:132
  168.0 4.7 %all-to-all-done.2 = f32[8,32,256]{2,1,0:T(8,128)S(1)} async-done(((f32[8,32,256]{2,1,0:T(8,128)}), f32[8,32,256]{2,1,0:T(8,128)S(1)}, u32[]{:S(2)}, u32[]{:S(2)}) %all-to-all-start.2) | async-done | bytes 262176 | tf_op jit(solution)/shard_map/all_to_all | solution.py:55
  172.9 3.7 %exponential_reduce_fusion = (f32[32]{0:T(128)S(1)}, f32[32,2048]{1,0:T(8,128)S(1)}) fusion(f32[32,256]{1,0:T(8,128)S(1)} %broadcast_multiply_fusion.1, f32[2048,256]{1,0:T(8,128)} %bitcast_multiply_fusion), kind=kOutput, calls=%fused_computation.78 | convolution fusion | flops 201457632 | bytes 2392192 | tf_op jit(solution)/shard_map/tq,bq->tb/dot_general | solution.py:156
  176.6 0.8 gather_fusion.3
  177.4 0.5 compare_select_fusion.5
  (50 shorter events, 1.1 us)
Async XLA Ops:
  0.6 115.5 %copy-start = (bf16[1536,1024]{1,0:T(8,128)(2,1)S(1)}, bf16[1536,1024]{1,0:T(8,128)(2,1)}, u32[]{:S(2)}) copy-start(bf16[1536,1024]{1,0:T(8,128)(2,1)} %param.18) | copy-start | bytes 9437188
  3.4 1.2 copy-start.2
  4.6 8.5 %copy-start.6 = (s32[4,4,32]{2,1,0:T(4,128)S(1)}, s32[4,4,32]{2,1,0:T(4,128)}, u32[]{:S(2)}) copy-start(s32[4,4,32]{2,1,0:T(4,128)} %param.20) | copy-start | bytes 6148
  4.6 8.8 %copy-start.9 = (s32[1,256]{1,0:T(1,128)S(1)}, s32[1,256]{1,0:T(1,128)}, u32[]{:S(2)}) copy-start(s32[1,256]{1,0:T(1,128)} %param.21) | copy-start | bytes 3076
  4.6 20.3 %copy-start.1 = (s32[4,64]{1,0:T(4,128)S(1)}, s32[4,64]{1,0:T(4,128)}, u32[]{:S(2)}) copy-start(s32[4,64]{1,0:T(4,128)} %param.22) | copy-start | bytes 3076
  4.6 21.1 %copy-start.7 = (bf16[1536]{0:T(1024)(128)(2,1)S(1)}, bf16[1536]{0:T(1024)(128)(2,1)}, u32[]{:S(2)}) copy-start(bf16[1536]{0:T(1024)(128)(2,1)} %param.14) | copy-start | bytes 9220
  4.6 21.1 %copy-start.8 = (bf16[1536]{0:T(1024)(128)(2,1)S(1)}, bf16[1536]{0:T(1024)(128)(2,1)}, u32[]{:S(2)}) copy-start(bf16[1536]{0:T(1024)(128)(2,1)} %param.17) | copy-start | bytes 9220
  4.6 39.6 %copy-start.10 = (bf16[7,7,1536]{2,1,0:T(8,128)(2,1)S(1)}, bf16[7,7,1536]{2,1,0:T(8,128)(2,1)}, u32[]{:S(2)}) copy-start(bf16[7,7,1536]{2,1,0:T(8,128)(2,1)} %param.13) | copy-start | bytes 451588
  6.7 37.5 %collective-permute-start = (bf16[4,3,32,1536]{3,0,2,1:T(4,128)(2,1)}, bf16[4,3,32,1536]{3,0,2,1:T(4,128)(2,1)}, u32[]{:S(2)}, u32[]{:S(2)}) collective-permute-start(bf16[4,3,32,1536]{3,0,2,1:T(4,128)(2,1)} %get-tuple-element.4), channel_id=1, source_target_pairs={{0,2},{2,4},{4,6},{6,8},{8,10},{10,12},{12,14},{1,3},{3,5},{5,7},{... | collective-permute-start | bytes 3538952 | tf_op jit(solution)/shard_map/ppermute | solution.py:36
  11.8 32.5 %collective-permute-start.1 = (bf16[4,3,32,1536]{3,0,2,1:T(4,128)(2,1)}, bf16[4,3,32,1536]{3,0,2,1:T(4,128)(2,1)}, u32[]{:S(2)}, u32[]{:S(2)}) collective-permute-start(bf16[4,3,32,1536]{3,0,2,1:T(4,128)(2,1)} %get-tuple-element.5), channel_id=1, source_target_pairs={{2,0},{4,2},{6,4},{8,6},{10,8},{12,10},{14,12},{3,1},{5,3},{7,5},{... | collective-permute-start | bytes 3538952 | tf_op jit(solution)/shard_map/ppermute | solution.py:37
  17.4 26.8 %all-to-all-start.3 = ((f32[8,1,32]{2,1,0:T(1,128)}), f32[8,1,32]{2,1,0:T(1,128)S(1)}, u32[]{:S(2)}, u32[]{:S(2)}) async-start(f32[8,1,32]{2,1,0:T(1,128)} %all_to_all.21), calls=%async_computation.3 | async-start | bytes 8192 | tf_op jit(solution)/shard_map/all_to_all | solution.py:55
  86.0 11.7 %copy-start.5 = (bf16[32,256]{1,0:T(8,128)(2,1)S(1)}, bf16[32,256]{1,0:T(8,128)(2,1)}, u32[]{:S(2)}) copy-start(bf16[32,256]{1,0:T(8,128)(2,1)} %param.23) | copy-start | bytes 49156
  98.9 26.3 %all-to-all-start.4 = ((bf16[64,32,256]{2,1,0:T(8,128)(2,1)}), bf16[64,32,256]{2,1,0:T(8,128)(2,1)}, u32[]{:S(2)}, u32[]{:S(2)}) async-start(bf16[64,32,256]{2,1,0:T(8,128)(2,1)} %broadcast_in_dim.39), calls=%async_computation.4 | async-start | bytes 2097152 | tf_op jit(solution)/shard_map/all_to_all | solution.py:22
  118.8 1.0 copy-start.3
  120.8 7.9 %collective-permute-start.2 = (bf16[4,1,32,1024]{3,0,2,1:T(4,128)(2,1)}, bf16[4,1,32,1024]{3,0,2,1:T(4,128)(2,1)S(1)}, u32[]{:S(2)}, u32[]{:S(2)}) collective-permute-start(bf16[4,1,32,1024]{3,0,2,1:T(4,128)(2,1)} %get-tuple-element.6), channel_id=1, source_target_pairs={{0,2},{2,4},{4,6},{6,8},{8,10},{10,12},{12,14},{1,3},{3,5},{5,7},{... | collective-permute-start | bytes 786440 | tf_op jit(solution)/shard_map/ppermute | solution.py:36
  123.7 8.9 %collective-permute-start.3 = (bf16[4,1,32,1024]{3,0,2,1:T(4,128)(2,1)}, bf16[4,1,32,1024]{3,0,2,1:T(4,128)(2,1)}, u32[]{:S(2)}, u32[]{:S(2)}) collective-permute-start(bf16[4,1,32,1024]{3,0,2,1:T(4,128)(2,1)} %get-tuple-element.7), channel_id=1, source_target_pairs={{2,0},{4,2},{6,4},{8,6},{10,8},{12,10},{14,12},{3,1},{5,3},{7,5},{... | collective-permute-start | bytes 786440 | tf_op jit(solution)/shard_map/ppermute | solution.py:37
  135.9 1.7 copy-start.11
  156.3 16.4 %all-to-all-start.2 = ((f32[8,32,256]{2,1,0:T(8,128)}), f32[8,32,256]{2,1,0:T(8,128)S(1)}, u32[]{:S(2)}, u32[]{:S(2)}) async-start(f32[8,32,256]{2,1,0:T(8,128)} %bitcast.48), calls=%async_computation.2 | async-start | bytes 524288 | tf_op jit(solution)/shard_map/all_to_all | solution.py:55
  172.9 5.0 %copy-start.4 = (f32[32,256]{1,0:T(8,128)}, f32[32,256]{1,0:T(8,128)S(1)}, u32[]{:S(2)}) copy-start(f32[32,256]{1,0:T(8,128)S(1)} %broadcast_multiply_fusion.1) | copy-start | bytes 98308
where the time goes:
time: 180 us; the launch traced here: 178 us
  matrix products  48.2 us (27%)
  starting transfers between devices  35.6 us (20%)
  waiting for transfers between devices  29 us (16%)
  local copies, waits for them, and re-layouts  23.4 us (13%)
  other arithmetic  21.7 us (12%)
  blocking collectives  18.9 us (10%)
    all_to_all x2, waiting for transfers between devices, sent_and_summed(): lax.all_to_all(in_blocks(shard, dim, length), axis, 0, 0, tiled=True)  23.1 us
    conv_general_dilated x1, matrix products, body(): lax.conv_general_dilated(padded, dw_kernel.reshape(7, 7, 1, channels), (1...  19.8 us
    all_to_all x2, blocking collectives, from_everyone(): return lax.all_to_all(copies, axis, split_axis=0, concat_axis=0, tiled=True)  18.9 us
    all_to_all x2, starting transfers between devices, sent_and_summed(): lax.all_to_all(in_blocks(shard, dim, length), axis, 0, 0, tiled=True)  16.2 us
    dot_general x1, matrix products, body(): jnp.dot(inner_act, w_reduce, preferred_element_type=jnp.float32)  15.9 us
    all_to_all x1, starting transfers between devices, from_everyone(): return lax.all_to_all(copies, axis, split_axis=0, concat_axis=0, tiled=True)  8.95 us
    ppermute x2, starting transfers between devices, padded_2(): before = lax.ppermute(last, axis, up)  7.9 us
    reduce_sum x2, other arithmetic, over_copies(): return jnp.sum(everything, axis=0)  7.58 us
  transfers between devices with their start and end apart: 7, of which 5 were waited for; matrix products, arithmetic and copies ran while one was open for 12% of the time, Pallas kernels for 0%

commit v1 on v0

v1 whole, which is shorter than its diff:
```python
import jax
import jax.numpy as jnp
from jax import lax
from jax.experimental import pallas as pl
from jax.experimental.pallas import tpu as pltpu
from jax.sharding import PartitionSpec as P

MESH = pl.DeviceIdType.MESH
REG = 64
LN_EPS = 1e-06
NORM_EPS = 1e-06
F32 = jnp.float32
BF16 = jnp.bfloat16


def split3(x):
    hi = x.astype(BF16)
    rest = x - hi.astype(F32)
    mid = rest.astype(BF16)
    lo = (rest - mid.astype(F32)).astype(BF16)
    return hi, mid, lo


def dot(a, b):
    return jnp.dot(a, b, preferred_element_type=F32)


def dot_t(a, b):
    return lax.dot_general(a, b, (((1,), (1,)), ((), ())), preferred_element_type=F32)


def gelu(x):
    return 0.5 * x * (1.0 + lax.erf(x * 0.7071067811865476))


def shifted(x, by, col):
    if by == 0:
        return x
    n = x.shape[0]
    moved = pltpu.roll(x, by % n, 0)
    keep = (col >= by) if by > 0 else (col < 32 + by)
    return jnp.where(keep, moved, 0.0)


def kernel(
    f, dwk, gain, w1, w2, scale, pe, pk, rid, own, par, key,
    emb_o, loss_o,
    fv, halo, dwv, dwf, w1v, w2v, pev, pkv, gv, sv, ownv, parv,
    taps, nrm, inner, bpart, bsend, brecv, bo, hid, acc, pooled, ordered, gathered, sibsum,
    rids, kall, knorm,
    lsem, hs, hr, ns, nr, bs, br, rs1, rr1, ks1, kr1, ks2, kr2, ks3, kr3, ps, pr, ss, sr,
):
    b = lax.axis_index("batch")
    r = lax.axis_index("rows")
    s = lax.axis_index("section")
    sib = (b, r, 1 - s)
    up = (b, jnp.maximum(r - 1, 0), s)
    down = (b, jnp.minimum(r + 1, 7), s)
    row_peer = [(b, lax.rem(r + d, 8), s) for d in range(1, 8)]
    batch_peer = [(lax.rem(b + d, 8), r, s) for d in range(1, 8)]

    barrier = pltpu.get_barrier_semaphore()
    for device in [sib] + row_peer + batch_peer:
        pl.semaphore_signal(barrier, inc=1, device_id=device, device_id_type=MESH)

    def local(src, dst, i):
        return pltpu.make_async_copy(src, dst, lsem.at[i])

    def remote(src, dst, send, recv, device):
        return pltpu.make_async_remote_copy(
            src_ref=src, dst_ref=dst, send_sem=send, recv_sem=recv, device_id=device, device_id_type=MESH
        )

    loads = {
        "f": local(f, fv, 0),
        "dw": local(dwk, dwv, 1),
        "rid": local(rid, rids.at[r], 2),
        "key": local(key, kall.at[b * 8 + r], 3),
        "own": local(own, ownv, 4),
        "par": local(par, parv, 5),
        "w1": local(w1, w1v, 6),
        "w2": local(w2, w2v, 7),
        "pe": local(pe, pev, 8),
        "pk": local(pk, pkv, 9),
        "gain": local(gain, gv, 10),
        "scale": local(scale, sv, 11),
    }
    for name in ("dw", "f", "gain", "scale", "rid", "key", "own", "par", "w1", "w2", "pe", "pk"):
        loads[name].start()

    pl.semaphore_wait(barrier, 15)

    def halo_up(i):
        return remote(f.at[2 * s + i, pl.ds(0, 3)], halo.at[i, 1], hs.at[i, 0], hr.at[i, 1], up)

    def halo_down(i):
        return remote(f.at[2 * s + i, pl.ds(1, 3)], halo.at[i, 0], hs.at[i, 1], hr.at[i, 0], down)

    for i in range(2):
        @pl.when(r > 0)
        def _():
            halo_up(i).start()

        @pl.when(r < 7)
        def _():
            halo_down(i).start()

    rid_copies = [
        remote(rid, rids.at[r], rs1.at[d], rr1.at[d], row_peer[d]) for d in range(7)
    ]
    key_rows = [
        remote(key, kall.at[b * 8 + r], ks1.at[d], kr1.at[d], row_peer[d]) for d in range(7)
    ]
    for copy in rid_copies + key_rows:
        copy.start()

    for i in range(2):
        @pl.when(r == 0)
        def _():
            halo[i, 0] = jnp.zeros_like(halo[i, 0])

        @pl.when(r == 7)
        def _():
            halo[i, 1] = jnp.zeros_like(halo[i, 1])

    loads["dw"].wait()
    for dy in range(7):
        dwf[dy, 0:7, :] = dwv[dy].astype(F32)
    loads["f"].wait()

    col32 = lax.broadcasted_iota(jnp.int32, (32, 128), 0)

    def conv_rows(i, lanes, rows, get, first):
        for y in range(4):
            sums = [None] * 7
            for yi in rows:
                dy = yi - y + 3
                if dy < 0 or dy > 6:
                    continue
                x = get(yi)
                for dx in range(7):
                    term = x * dwf[dy, dx : dx + 1, lanes]
                    sums[dx] = term if sums[dx] is None else sums[dx] + term
            total = sums[3]
            for dx in (0, 1, 2, 4, 5, 6):
                total = total + shifted(sums[dx], 3 - dx, col32)
            if first:
                taps[i, y, :, lanes] = total
            else:
                taps[i, y, :, lanes] = taps[i, y, :, lanes] + total

    def own_part(n, _):
        i = n // 12
        lanes = pl.ds(pl.multiple_of((n % 12) * 128, 128), 128)
        xs = [fv[2 * s + i, y, :, lanes].astype(F32) for y in range(4)]
        conv_rows(i, lanes, range(4), lambda yi: xs[yi], True)
        return 0

    lax.fori_loop(0, 24, own_part, 0)

    def halo_part(i):
        def step(n, _):
            lanes = pl.ds(pl.multiple_of(n * 128, 128), 128)
            xs = {}
            for k in range(3):
                xs[k - 3] = halo[i, 0, k, :, lanes].astype(F32)
                xs[4 + k] = halo[i, 1, k, :, lanes].astype(F32)
            conv_rows(i, lanes, (-3, -2, -1, 4, 5, 6), lambda yi: xs[yi], False)
            return 0

        lax.fori_loop(0, 12, step, 0)

    def layer_norm(i):
        def step(y, _):
            t = taps[i, y]
            mean = jnp.sum(t, axis=-1, keepdims=True) * (1.0 / 1536)
            t = t - mean
            spread = jnp.sum(t * t, axis=-1, keepdims=True) * (1.0 / 1536)
            out = t * lax.rsqrt(spread + LN_EPS) * gv[...].astype(F32)
            nrm[i, s, pl.ds(pl.multiple_of(y * 32, 32), 32), :] = out.astype(BF16)
            return 0

        lax.fori_loop(0, 4, step, 0)

    def norm_copy(i):
        return remote(nrm.at[i, s], nrm.at[i, s], ns.at[i], nr.at[i], sib)

    def branch_copy(i, n):
        return remote(bsend.at[i, n], brecv.at[i, n], bs.at[i, n], br.at[i, n], sib)

    def wait_halo(i):
        @pl.when(r > 0)
        def _():
            halo_up(i).wait_send()
            halo_down(i).wait_recv()

        @pl.when(r < 7)
        def _():
            halo_down(i).wait_send()
            halo_up(i).wait_recv()

    def mlp(i):
        x = nrm.at[i]

        def up_tile(n, _):
            lanes = pl.ds(pl.multiple_of(n * 256, 256), 256)
            h = dot(x[...].reshape(256, 1536), w1v[:, lanes])
            inner[:, lanes] = gelu(h).astype(BF16)
            return 0

        lax.fori_loop(0, 6, up_tile, 0)

        def down_tile(n, _):
            lanes = pl.ds(pl.multiple_of(n * 256, 256), 256)
            h = dot(inner[...], w2v[:, lanes])
            bpart[n] = h
            bsend[i, n] = h.astype(BF16)
            branch_copy(i, n).start()
            return 0

        lax.fori_loop(0, 6, down_tile, 0)

    col192 = lax.broadcasted_iota(jnp.int32, (192, 256), 0) % 32

    def project(i):
        def merge_tile(n, _):
            lanes = pl.ds(pl.multiple_of(n * 256, 256), 256)
            branch_copy(i, n).wait()
            sc = sv[:, lanes].astype(F32)
            for h in range(2):
                rows = slice(128 * h, 128 * h + 128)
                base = fv[2 * h + i, :, :, lanes].reshape(128, 256).astype(F32)
                total = bpart[n, rows, :] + brecv[i, n, rows, :].astype(F32)
                bo[rows, lanes] = (base + sc * total).astype(BF16)
            return 0

        lax.fori_loop(0, 6, merge_tile, 0)

        def expand_tile(n, _):
            lanes = pl.ds(pl.multiple_of(n * 256, 256), 256)
            h = dot(bo[...], pev[:, lanes])
            hid[:, lanes] = jnp.maximum(h, 0.0).astype(BF16)
            return 0

        lax.fori_loop(0, 4, expand_tile, 0)

        acc[...] = jnp.zeros_like(acc)

        def tap(n, _):
            dy = n // 3
            dx = n % 3
            h = dot(hid[...], pkv[n])
            rows = pl.ds(pl.multiple_of((2 - dy) * 32, 32), 128)
            for k in range(2):
                acc[k, dx, rows, :] = acc[k, dx, rows, :] + h[128 * k : 128 * k + 128]
            return 0

        lax.fori_loop(0, 9, tap, 0)

        reg = lax.broadcasted_iota(jnp.int32, (REG, 192), 0)
        for k in range(2):
            img = 2 * k + i
            total = shifted(acc[k, 0], 1, col192) + acc[k, 1] + shifted(acc[k, 2], -1, col192)
            above = jnp.where(r > 0, rids[jnp.maximum(r - 1, 0), img, 3:4, :], -1)
            below = jnp.where(r < 7, rids[jnp.minimum(r + 1, 7), img, 0:1, :], -1)
            ids = jnp.concatenate(
                [above] + [rids[r, img, y : y + 1, :] for y in range(4)] + [below], axis=1
            )
            onehot = jnp.where(reg == ids, 1.0, 0.0).astype(BF16)
            hi, mid, lo = split3(total)
            pooled[64 * img : 64 * img + 64, :] = dot(onehot, hi) + dot(onehot, mid) + dot(onehot, lo)

    for copy in rid_copies:
        copy.wait()
    loads["rid"].wait()
    loads["gain"].wait()
    loads["scale"].wait()

    wait_halo(0)
    halo_part(0)
    layer_norm(0)
    norm_copy(0).start()
    loads["w1"].wait()
    loads["w2"].wait()

    for copy in key_rows:
        copy.wait()
    loads["key"].wait()
    half = pl.ds(b * 8 + 4 * s, 4)
    key_batch = [
        remote(kall.at[half], kall.at[half], ks2.at[d], kr2.at[d], batch_peer[d]) for d in range(7)
    ]
    for copy in key_batch:
        copy.start()

    norm_copy(0).wait()
    mlp(0)
    loads["pe"].wait()
    loads["pk"].wait()
    project(0)

    wait_halo(1)
    halo_part(1)
    layer_norm(1)
    norm_copy(1).start()
    for copy in key_batch:
        copy.wait()
    key_sib = []
    for d in range(1, 8):
        part = pl.ds(lax.rem(b + 8 - d, 8) * 8 + 4 * s, 4)
        key_sib.append(remote(kall.at[part], kall.at[part], ks3.at[d], kr3.at[d], sib))
    for copy in key_sib:
        copy.start()
    norm_copy(1).wait()
    mlp(1)
    project(1)

    loads["own"].wait()
    loads["par"].wait()
    place = lax.broadcasted_iota(jnp.int32, (256, 256), 0)
    perm = jnp.where(place == ownv[...], 1.0, 0.0).astype(BF16)
    hi, mid, lo = split3(pooled[...])
    ordered[...] = (dot(perm, hi) + dot(perm, mid) + dot(perm, lo)).reshape(8, 32, 256)
    pool_copies = [
        remote(ordered.at[lax.rem(r + d, 8)], gathered.at[d], ps.at[d], pr.at[d], row_peer[d - 1])
        for d in range(1, 8)
    ]
    for copy in pool_copies:
        copy.start()

    for copy in key_sib:
        copy.wait()

    ones = jnp.ones((8, 256), BF16)

    def key_norms(n, _):
        k = kall[pl.ds(n * 8, 8)].reshape(256, 256).astype(F32)
        sq = k * k
        top = sq.astype(BF16)
        bottom = (sq - top.astype(F32)).astype(BF16)
        total = dot_t(ones, top) + dot_t(ones, bottom)
        knorm[:, pl.ds(pl.multiple_of(n * 256, 256), 256)] = lax.rsqrt(total + NORM_EPS) * 10.0
        return 0

    lax.fori_loop(0, 8, key_norms, 0)

    slot = lax.broadcasted_iota(jnp.int32, (1, 256), 1)
    partner = jnp.concatenate([parv[k : k + 1, :] for k in range(4)], axis=1)
    positive = (slot // REG * REG + b * 256 + partner).astype(F32)
    used = jnp.zeros((1, 256), F32)
    for k in range(4):
        ids = jnp.max(rids[:, k].astype(F32), axis=0)
        most = jnp.max(jnp.max(ids, axis=1, keepdims=True), axis=0, keepdims=True)
        here = (slot // REG == k) & ((slot % REG).astype(F32) <= most)
        used = jnp.where(here, 1.0, used)
    mine = (lax.broadcasted_iota(jnp.int32, (32, 256), 0) + 32 * r) == ownv[...]
    pos = jnp.sum(jnp.where(mine, positive, 0.0), axis=1, keepdims=True)
    ok = jnp.sum(jnp.where(mine, used, 0.0), axis=1, keepdims=True)

    for copy in pool_copies:
        copy.wait()
    total = ordered[r]
    for d in range(1, 8):
        total = total + gathered[d]
    sibsum[0] = total
    sib_copy = remote(sibsum.at[0], sibsum.at[1], ss.at[0], sr.at[0], sib)
    sib_copy.start()
    sib_copy.wait()
    total = sibsum[0] + sibsum[1]
    probe = total * lax.rsqrt(jnp.sum(total * total, axis=1, keepdims=True) + NORM_EPS)
    emb_o[...] = probe
    hi, mid, lo = split3(probe)
    keys = kall[...].reshape(2048, 256)
    logits = (dot_t(hi, keys) + dot_t(mid, keys) + dot_t(lo, keys)) * knorm[0:1, :]
    sums = jnp.log(jnp.sum(jnp.exp(logits), axis=1, keepdims=True))
    index = lax.broadcasted_iota(jnp.int32, (32, 2048), 1).astype(F32)
    pos_logit = jnp.sum(jnp.where(index == pos, logits, 0.0), axis=1, keepdims=True)
    loss = jnp.where(ok > 0.5, sums - pos_logit, 0.0)
    eye = lax.broadcasted_iota(jnp.int32, (32, 32), 0) == lax.broadcasted_iota(jnp.int32, (32, 32), 1)
    loss_o[...] = jnp.sum(jnp.where(eye, loss, 0.0), axis=0, keepdims=True)


def body(*args):
    args = list(args)
    args[2] = args[2].reshape(1, -1)
    args[5] = args[5].reshape(1, -1)
    dma = pltpu.SemaphoreType.DMA
    vmem = pltpu.VMEM
    scratch = [
        vmem((4, 4, 32, 1536), BF16),
        vmem((2, 2, 3, 32, 1536), BF16),
        vmem((7, 7, 1536), BF16),
        vmem((7, 8, 1536), F32),
        vmem((1536, 1536), BF16),
        vmem((1536, 1536), BF16),
        vmem((1536, 1024), BF16),
        vmem((9, 1024, 256), BF16),
        vmem((1, 1536), BF16),
        vmem((1, 1536), BF16),
        vmem((1, 256), jnp.int32),
        vmem((4, 64), jnp.int32),
        vmem((2, 4, 32, 1536), F32),
        vmem((2, 2, 128, 1536), BF16),
        vmem((256, 1536), BF16),
        vmem((6, 256, 256), F32),
        vmem((2, 6, 256, 256), BF16),
        vmem((2, 6, 256, 256), BF16),
        vmem((256, 1536), BF16),
        vmem((256, 1024), BF16),
        vmem((2, 3, 192, 256), F32),
        vmem((256, 256), F32),
        vmem((8, 32, 256), F32),
        vmem((8, 32, 256), F32),
        vmem((2, 32, 256), F32),
        vmem((8, 4, 4, 32), jnp.int32),
        vmem((64, 32, 256), BF16),
        vmem((8, 2048), F32),
        dma((12,)),
        dma((2, 2)), dma((2, 2)),
        dma((2,)), dma((2,)),
        dma((2, 6)), dma((2, 6)),
        dma((8,)), dma((8,)),
        dma((8,)), dma((8,)),
        dma((8,)), dma((8,)),
        dma((8,)), dma((8,)),
        dma((8,)), dma((8,)),
        dma((1,)), dma((1,)),
    ]
    emb, loss = pl.pallas_call(
        kernel,
        out_shape=(
            jax.ShapeDtypeStruct((32, 256), F32),
            jax.ShapeDtypeStruct((1, 32), F32),
        ),
        in_specs=[pl.BlockSpec(memory_space=pl.ANY)] * 12,
        out_specs=(pl.BlockSpec(memory_space=pltpu.VMEM), pl.BlockSpec(memory_space=pltpu.VMEM)),
        scratch_shapes=scratch,
        compiler_params=pltpu.CompilerParams(
            collective_id=0, has_side_effects=True, vmem_limit_bytes=60 * 1024 * 1024
        ),
        name="region_loss",
    )(*args)
    return emb, loss.reshape(32)


def solution(mesh):
    in_specs = (
        P("batch", "rows", None, None),
        P(),
        P(),
        P(None, "section"),
        P("section", None),
        P(),
        P(None, "section"),
        P(None, "section", None),
        P("batch", "rows", None),
        P("batch", None),
        P("batch", None),
        P(("batch", "rows"), None),
    )
    out_specs = (P(("batch", "rows"), None), P(("batch", "rows")))
    return jax.shard_map(body, mesh=mesh, in_specs=in_specs, out_specs=out_specs, check_vma=False)
```

time: 180 us -> 69.7 us (0.39); the launches traced: 178 us -> 69.5 us
  Pallas kernels: 0 us -> 63.8 us
  matrix products: 48.2 us -> 0 us
  starting transfers between devices: 35.6 us -> 0 us
  waiting for transfers between devices: 29 us -> 0 us
  other arithmetic: 21.7 us -> 0 us
  blocking collectives: 18.9 us -> 0 us
  local copies, waits for them, and re-layouts: 23.4 us -> 5.09 us
    pallas_call x0 -> x1, Pallas kernels: none -> 63.8 us  [body(): pl.pallas_call(kernel, out_shape=(jax.ShapeDtypeStruct((32, 256), F32), j...]
    conv_general_dilated x2 -> x0, matrix products: 25.4 us -> none  [the longest x1 19.8 us: body(): lax.conv_general_dilated(padded, dw_kernel.reshape(7, 7, 1, channels), (1...]
    all_to_all x3 -> x0, starting transfers between devices: 25.1 us -> none  [the longest x2 16.2 us: sent_and_summed(): lax.all_to_all(in_blocks(shard, dim, length), axis, 0, 0, tiled=True)]
    all_to_all x3 -> x0, waiting for transfers between devices: 23.4 us -> none  [the longest x2 23.1 us: sent_and_summed(): lax.all_to_all(in_blocks(shard, dim, length), axis, 0, 0, tiled=True)]
    dot_general x4 -> x0, matrix products: 22.8 us -> none  [the longest x1 15.9 us: body(): jnp.dot(inner_act, w_reduce, preferred_element_type=jnp.float32)]
    all_to_all x2 -> x0, blocking collectives: 18.9 us -> none  [from_everyone(): return lax.all_to_all(copies, axis, split_axis=0, concat_axis=0, tiled=True)]
    ppermute x4 -> x0, starting transfers between devices: 10.5 us -> none  [the longest x2 7.9 us: padded_2(): before = lax.ppermute(last, axis, up)]
    reduce_sum x8 -> x0, other arithmetic: 10.4 us -> none  [the longest x2 7.58 us: over_copies(): return jnp.sum(everything, axis=0)]
  transfers between devices with their start and end apart: 7 -> 0, of which waited for: 5 -> 0; matrix products, arithmetic and copies ran while one was open for 12% -> 0% of each run, Pallas kernels for 0% -> 0%
where the time goes in v1:
time: 69.7 us; the launch traced here: 69.5 us
  Pallas kernels  63.8 us (92%)
  local copies, waits for them, and re-layouts  5.09 us (7%)
    pallas_call x1, Pallas kernels, body(): pl.pallas_call(kernel, out_shape=(jax.ShapeDtypeStruct((32, 256), F32), j...  63.8 us
    unnamed x2, local copies, waits for them, and re-layouts  2.52 us

profile of v1, /device:TPU:1, one launch (start us, length us, event | category | flops | bytes accessed | tf_op | source)
XLA Modules:
  0.0 69.5 jit_solution(4065551776430443896)
XLA Ops:
  0.6 1.3 %reshape.13.gain = bf16[1,1536]{1,0:T(2,128)(2,1)} reshape(bf16[1536]{0:T(1024)(128)(2,1)} %param.14) | data formatting | bytes 6144 | tf_op jit(solution)/shard_map/reshape | solution.py:385
  1.9 1.3 %reshape.14.scale = bf16[1,1536]{1,0:T(2,128)(2,1)} reshape(bf16[1536]{0:T(1024)(128)(2,1)} %param.17) | data formatting | bytes 6144 | tf_op jit(solution)/shard_map/reshape | solution.py:386
  3.2 63.8 %region_loss.1 = (f32[32,256]{1,0:T(8,128)}, f32[1,32]{1,0:T(1,128)}) custom-call(bf16[4,4,32,1536]{3,2,1,0:T(8,128)(2,1)} %f.1, bf16[7,7,1536]{2,1,0:T(8,128)(2,1)} %dwk.1, bf16[1,1536]{1,0:T(2,128)(2,1)} %reshape.13.gain, bf16[1536,1536]{1,0:T(8,128)(2,1)} %w1.1, bf16[1536,1536]{1,0:T(8,128)(2,1)} %w2.1, bf16[1,1536]{1,0:T(2,128)(2,1)} %reshape.14.scale, ...), custom_call_target="tpu_custom_call" | custom-call | tf_op jit(solution)/shard_map/region_loss/pallas_call | solution.py:429
  67.0 1.4 %copy.16 = f32[32,256]{1,0:T(8,128)} copy(f32[32,256]{1,0:T(8,128)} %get-tuple-element.8) | data formatting | bytes 65536
  68.4 1.1 %copy.17 = f32[32]{0:T(128)} copy(f32[32]{0:T(128)} %bitcast.1) | data formatting | bytes 256

commit v2 on v1

--- a/solution.py
+++ b/solution.py
@@ -96,7 +96,7 @@
     def halo_down(i):
         return remote(f.at[2 * s + i, pl.ds(1, 3)], halo.at[i, 0], hs.at[i, 1], hr.at[i, 0], down)
 
-    for i in range(2):
+    def start_halo(i):
         @pl.when(r > 0)
         def _():
             halo_up(i).start()
@@ -104,6 +104,17 @@
         @pl.when(r < 7)
         def _():
             halo_down(i).start()
+
+    def halo_sent(i):
+        @pl.when(r > 0)
+        def _():
+            halo_up(i).wait_send()
+
+        @pl.when(r < 7)
+        def _():
+            halo_down(i).wait_send()
+
+    start_halo(0)
 
     rid_copies = [
         remote(rid, rids.at[r], rs1.at[d], rr1.at[d], row_peer[d]) for d in range(7)
@@ -157,6 +168,8 @@
         return 0
 
     lax.fori_loop(0, 24, own_part, 0)
+    halo_sent(0)
+    start_halo(1)
 
     def halo_part(i):
         def step(n, _):
@@ -176,7 +189,7 @@
             mean = jnp.sum(t, axis=-1, keepdims=True) * (1.0 / 1536)
             t = t - mean
             spread = jnp.sum(t * t, axis=-1, keepdims=True) * (1.0 / 1536)
-            out = t * lax.rsqrt(spread + LN_EPS) * gv[...].astype(F32)
+            out = t * lax.rsqrt(spread + LN_EPS) * gv[...].astype(F32).reshape(1, 1536)
             nrm[i, s, pl.ds(pl.multiple_of(y * 32, 32), 32), :] = out.astype(BF16)
             return 0
 
@@ -185,48 +198,39 @@
     def norm_copy(i):
         return remote(nrm.at[i, s], nrm.at[i, s], ns.at[i], nr.at[i], sib)
 
-    def branch_copy(i, n):
-        return remote(bsend.at[i, n], brecv.at[i, n], bs.at[i, n], br.at[i, n], sib)
+    def branch_copy(i, half):
+        part = pl.ds(3 * half, 3)
+        return remote(bsend.at[i, part], brecv.at[i, part], bs.at[i, half], br.at[i, half], sib)
 
     def wait_halo(i):
         @pl.when(r > 0)
         def _():
-            halo_up(i).wait_send()
             halo_down(i).wait_recv()
 
         @pl.when(r < 7)
         def _():
-            halo_down(i).wait_send()
             halo_up(i).wait_recv()
 
+    def tile(n):
+        return slice(256 * n, 256 * n + 256)
+
     def mlp(i):
-        x = nrm.at[i]
-
-        def up_tile(n, _):
-            lanes = pl.ds(pl.multiple_of(n * 256, 256), 256)
-            h = dot(x[...].reshape(256, 1536), w1v[:, lanes])
-            inner[:, lanes] = gelu(h).astype(BF16)
-            return 0
-
-        lax.fori_loop(0, 6, up_tile, 0)
-
-        def down_tile(n, _):
-            lanes = pl.ds(pl.multiple_of(n * 256, 256), 256)
-            h = dot(inner[...], w2v[:, lanes])
-            bpart[n] = h
-            bsend[i, n] = h.astype(BF16)
-            branch_copy(i, n).start()
-            return 0
-
-        lax.fori_loop(0, 6, down_tile, 0)
+        x = nrm[i].reshape(256, 1536)
+        for n in range(6):
+            inner[:, tile(n)] = gelu(dot(x, w1v[:, tile(n)])).astype(BF16)
+        for half in range(2):
+            for n in range(3 * half, 3 * half + 3):
+                h = dot(inner[...], w2v[:, tile(n)])
+                bpart[n] = h
+                bsend[i, n] = h.astype(BF16)
+            branch_copy(i, half).start()
 
     col192 = lax.broadcasted_iota(jnp.int32, (192, 256), 0) % 32
 
-    def project(i):
+    def merge(i):
         def merge_tile(n, _):
             lanes = pl.ds(pl.multiple_of(n * 256, 256), 256)
-            branch_copy(i, n).wait()
-            sc = sv[:, lanes].astype(F32)
+            sc = sv[lanes].astype(F32).reshape(1, 256)
             for h in range(2):
                 rows = slice(128 * h, 128 * h + 128)
                 base = fv[2 * h + i, :, :, lanes].reshape(128, 256).astype(F32)
@@ -234,28 +238,22 @@
                 bo[rows, lanes] = (base + sc * total).astype(BF16)
             return 0
 
-        lax.fori_loop(0, 6, merge_tile, 0)
-
-        def expand_tile(n, _):
-            lanes = pl.ds(pl.multiple_of(n * 256, 256), 256)
-            h = dot(bo[...], pev[:, lanes])
-            hid[:, lanes] = jnp.maximum(h, 0.0).astype(BF16)
-            return 0
-
-        lax.fori_loop(0, 4, expand_tile, 0)
-
+        for half in range(2):
+            branch_copy(i, half).wait()
+            lax.fori_loop(3 * half, 3 * half + 3, merge_tile, 0)
+
+    def expand(i):
+        for n in range(4):
+            hid[:, tile(n)] = jnp.maximum(dot(bo[...], pev[:, tile(n)]), 0.0).astype(BF16)
+
+    def project(i):
         acc[...] = jnp.zeros_like(acc)
-
-        def tap(n, _):
-            dy = n // 3
-            dx = n % 3
+        for n in range(9):
+            dy, dx = divmod(n, 3)
             h = dot(hid[...], pkv[n])
-            rows = pl.ds(pl.multiple_of((2 - dy) * 32, 32), 128)
+            rows = slice((2 - dy) * 32, (2 - dy) * 32 + 128)
             for k in range(2):
                 acc[k, dx, rows, :] = acc[k, dx, rows, :] + h[128 * k : 128 * k + 128]
-            return 0
-
-        lax.fori_loop(0, 9, tap, 0)
 
         reg = lax.broadcasted_iota(jnp.int32, (REG, 192), 0)
         for k in range(2):
@@ -295,24 +293,29 @@
 
     norm_copy(0).wait()
     mlp(0)
-    loads["pe"].wait()
-    loads["pk"].wait()
-    project(0)
 
     wait_halo(1)
+    halo_sent(1)
     halo_part(1)
     layer_norm(1)
     norm_copy(1).start()
+    loads["pe"].wait()
+    loads["pk"].wait()
+    merge(0)
+    expand(0)
+    norm_copy(1).wait()
+    mlp(1)
+    project(0)
     for copy in key_batch:
         copy.wait()
     key_sib = []
     for d in range(1, 8):
         part = pl.ds(lax.rem(b + 8 - d, 8) * 8 + 4 * s, 4)
         key_sib.append(remote(kall.at[part], kall.at[part], ks3.at[d], kr3.at[d], sib))
+    merge(1)
     for copy in key_sib:
         copy.start()
-    norm_copy(1).wait()
-    mlp(1)
+    expand(1)
     project(1)
 
     loads["own"].wait()
@@ -371,7 +374,8 @@
     emb_o[...] = probe
     hi, mid, lo = split3(probe)
     keys = kall[...].reshape(2048, 256)
-    logits = (dot_t(hi, keys) + dot_t(mid, keys) + dot_t(lo, keys)) * knorm[0:1, :]
+    parts = dot_t(jnp.concatenate([hi, mid, lo], axis=0), keys)
+    logits = (parts[0:32] + parts[32:64] + parts[64:96]) * knorm[0:1, :]
     sums = jnp.log(jnp.sum(jnp.exp(logits), axis=1, keepdims=True))
     index = lax.broadcasted_iota(jnp.int32, (32, 2048), 1).astype(F32)
     pos_logit = jnp.sum(jnp.where(index == pos, logits, 0.0), axis=1, keepdims=True)
@@ -380,10 +384,12 @@
     loss_o[...] = jnp.sum(jnp.where(eye, loss, 0.0), axis=0, keepdims=True)
 
 
+def finish(emb, loss, emb_o, loss_o):
+    emb_o[...] = emb[...]
+    loss_o[...] = loss[...]
+
+
 def body(*args):
-    args = list(args)
-    args[2] = args[2].reshape(1, -1)
-    args[5] = args[5].reshape(1, -1)
     dma = pltpu.SemaphoreType.DMA
     vmem = pltpu.VMEM
     scratch = [
@@ -395,8 +401,8 @@
         vmem((1536, 1536), BF16),
         vmem((1536, 1024), BF16),
         vmem((9, 1024, 256), BF16),
-        vmem((1, 1536), BF16),
-        vmem((1, 1536), BF16),
+        vmem((1536,), BF16),
+        vmem((1536,), BF16),
         vmem((1, 256), jnp.int32),
         vmem((4, 64), jnp.int32),
         vmem((2, 4, 32, 1536), F32),
@@ -418,7 +424,7 @@
         dma((12,)),
         dma((2, 2)), dma((2, 2)),
         dma((2,)), dma((2,)),
-        dma((2, 6)), dma((2, 6)),
+        dma((2, 2)), dma((2, 2)),
         dma((8,)), dma((8,)),
         dma((8,)), dma((8,)),
         dma((8,)), dma((8,)),
@@ -440,6 +446,16 @@
         ),
         name="region_loss",
     )(*args)
+    emb, loss = pl.pallas_call(
+        finish,
+        out_shape=(
+            jax.ShapeDtypeStruct((32, 256), F32),
+            jax.ShapeDtypeStruct((1, 32), F32),
+        ),
+        in_specs=[pl.BlockSpec(memory_space=pltpu.VMEM)] * 2,
+        out_specs=(pl.BlockSpec(memory_space=pltpu.VMEM), pl.BlockSpec(memory_space=pltpu.VMEM)),
+        name="finish",
+    )(emb, loss)
     return emb, loss.reshape(32)
 
 

time: 69.7 us -> 50.6 us (0.73)
  Pallas kernels: 63.8 us -> 49.8 us
  local copies, waits for them, and re-layouts: 5.09 us -> 0 us
    pallas_call x1, Pallas kernels: 63.8 us -> 48.4 us  [body(): pl.pallas_call(kernel, out_shape=(jax.ShapeDtypeStruct((32, 256), F32), j...]
    reshape x2 -> x0, local copies, waits for them, and re-layouts: 2.57 us -> none  [the longest x1 1.28 us: body(): args[2] = args[2].reshape(1, -1)]
    unnamed x2 -> x0, local copies, waits for them, and re-layouts: 2.52 us -> none
    pallas_call x0 -> x1, Pallas kernels: none -> 1.38 us  [body(): pl.pallas_call(finish, out_shape=(jax.ShapeDtypeStruct((32, 256), F32), j...]
where the time goes in v2:
time: 50.6 us; the launch traced here: 50.5 us
  Pallas kernels  49.8 us (98%)
  between operations  0.64 us (1%)
    pallas_call x1, Pallas kernels, body(): pl.pallas_call(kernel, out_shape=(jax.ShapeDtypeStruct((32, 256), F32), j...  48.4 us
    pallas_call x1, Pallas kernels, body(): pl.pallas_call(finish, out_shape=(jax.ShapeDtypeStruct((32, 256), F32), j...  1.38 us

profile of v2, /device:TPU:1, one launch (start us, length us, event | category | flops | bytes accessed | tf_op | source)
XLA Modules:
  0.0 50.5 jit_solution(14194506866069655020)
XLA Ops:
  0.6 48.4 %region_loss.1 = (f32[32,256]{1,0:T(8,128)}, f32[1,32]{1,0:T(1,128)}) custom-call(bf16[4,4,32,1536]{3,2,1,0:T(8,128)(2,1)} %f.1, bf16[7,7,1536]{2,1,0:T(8,128)(2,1)} %dwk.1, bf16[1536]{0:T(1024)(128)(2,1)} %gain.1, bf16[1536,1536]{1,0:T(8,128)(2,1)} %w1.1, bf16[1536,1536]{1,0:T(8,128)(2,1)} %w2.1, bf16[1536]{0:T(1024)(128)(2,1)} %scale.1, ...), custom_call_target="tpu_custom_call" | custom-call | tf_op jit(solution)/shard_map/region_loss/pallas_call | solution.py:435
  49.1 1.4 %finish.1 = (f32[32,256]{1,0:T(8,128)}, f32[1,32]{1,0:T(1,128)}) custom-call(f32[32,256]{1,0:T(8,128)} %get-tuple-element.6.emb, f32[1,32]{1,0:T(1,128)} %get-tuple-element.7.loss), custom_call_target="tpu_custom_call" | custom-call | tf_op jit(solution)/shard_map/finish/pallas_call | solution.py:449

commit v3 on v2

--- a/solution.py
+++ b/solution.py
@@ -46,9 +46,9 @@
     f, dwk, gain, w1, w2, scale, pe, pk, rid, own, par, key,
     emb_o, loss_o,
     fv, halo, dwv, dwf, w1v, w2v, pev, pkv, gv, sv, ownv, parv,
-    taps, nrm, inner, bpart, bsend, brecv, bo, hid, acc, pooled, ordered, gathered, sibsum,
+    taps, nrm, inner, bpart, bsend, brecv, bo, hid, acc, spot, ordered, ordered16, gathered,
     rids, kall, knorm,
-    lsem, hs, hr, ns, nr, bs, br, rs1, rr1, ks1, kr1, ks2, kr2, ks3, kr3, ps, pr, ss, sr,
+    lsem, hs, hr, ns, nr, bs, br, rs1, rr1, ks1, kr1, ks2, kr2, ks3, kr3, ps, pr,
 ):
     b = lax.axis_index("batch")
     r = lax.axis_index("rows")
@@ -57,10 +57,11 @@
     up = (b, jnp.maximum(r - 1, 0), s)
     down = (b, jnp.minimum(r + 1, 7), s)
     row_peer = [(b, lax.rem(r + d, 8), s) for d in range(1, 8)]
+    cross_peer = [(b, lax.rem(r + d, 8), 1 - s) for d in range(1, 8)]
     batch_peer = [(lax.rem(b + d, 8), r, s) for d in range(1, 8)]
 
     barrier = pltpu.get_barrier_semaphore()
-    for device in [sib] + row_peer + batch_peer:
+    for device in [sib] + row_peer + cross_peer + batch_peer:
         pl.semaphore_signal(barrier, inc=1, device_id=device, device_id_type=MESH)
 
     def local(src, dst, i):
@@ -88,43 +89,47 @@
     for name in ("dw", "f", "gain", "scale", "rid", "key", "own", "par", "w1", "w2", "pe", "pk"):
         loads[name].start()
 
-    pl.semaphore_wait(barrier, 15)
-
-    def halo_up(i):
-        return remote(f.at[2 * s + i, pl.ds(0, 3)], halo.at[i, 1], hs.at[i, 0], hr.at[i, 1], up)
-
-    def halo_down(i):
-        return remote(f.at[2 * s + i, pl.ds(1, 3)], halo.at[i, 0], hs.at[i, 1], hr.at[i, 0], down)
-
-    def start_halo(i):
+    pl.semaphore_wait(barrier, 22)
+
+    def halo_up(i, h):
+        lanes = pl.ds(768 * h, 768)
+        return remote(
+            f.at[2 * s + i, pl.ds(0, 3), :, lanes], halo.at[i, 1, :, :, lanes],
+            hs.at[i, 0, h], hr.at[i, 1, h], up,
+        )
+
+    def halo_down(i, h):
+        lanes = pl.ds(768 * h, 768)
+        return remote(
+            f.at[2 * s + i, pl.ds(1, 3), :, lanes], halo.at[i, 0, :, :, lanes],
+            hs.at[i, 1, h], hr.at[i, 0, h], down,
+        )
+
+    def start_halo(i, h):
         @pl.when(r > 0)
         def _():
-            halo_up(i).start()
+            halo_up(i, h).start()
 
         @pl.when(r < 7)
         def _():
-            halo_down(i).start()
-
-    def halo_sent(i):
+            halo_down(i, h).start()
+
+    def halo_sent(i, h):
         @pl.when(r > 0)
         def _():
-            halo_up(i).wait_send()
+            halo_up(i, h).wait_send()
 
         @pl.when(r < 7)
         def _():
-            halo_down(i).wait_send()
-
-    start_halo(0)
-
+            halo_down(i, h).wait_send()
+
+    start_halo(0, 0)
     rid_copies = [
         remote(rid, rids.at[r], rs1.at[d], rr1.at[d], row_peer[d]) for d in range(7)
     ]
     key_rows = [
         remote(key, kall.at[b * 8 + r], ks1.at[d], kr1.at[d], row_peer[d]) for d in range(7)
     ]
-    for copy in rid_copies + key_rows:
-        copy.start()
-
     for i in range(2):
         @pl.when(r == 0)
         def _():
@@ -167,11 +172,11 @@
         conv_rows(i, lanes, range(4), lambda yi: xs[yi], True)
         return 0
 
-    lax.fori_loop(0, 24, own_part, 0)
-    halo_sent(0)
-    start_halo(1)
-
-    def halo_part(i):
+    lax.fori_loop(0, 12, own_part, 0)
+    start_halo(0, 1)
+    lax.fori_loop(12, 24, own_part, 0)
+
+    def halo_part(i, part):
         def step(n, _):
             lanes = pl.ds(pl.multiple_of(n * 128, 128), 128)
             xs = {}
@@ -181,7 +186,7 @@
             conv_rows(i, lanes, (-3, -2, -1, 4, 5, 6), lambda yi: xs[yi], False)
             return 0
 
-        lax.fori_loop(0, 12, step, 0)
+        lax.fori_loop(6 * part, 6 * part + 6, step, 0)
 
     def layer_norm(i):
         def step(y, _):
@@ -193,23 +198,26 @@
             nrm[i, s, pl.ds(pl.multiple_of(y * 32, 32), 32), :] = out.astype(BF16)
             return 0
 
-        lax.fori_loop(0, 4, step, 0)
-
-    def norm_copy(i):
-        return remote(nrm.at[i, s], nrm.at[i, s], ns.at[i], nr.at[i], sib)
+        for part in range(2):
+            lax.fori_loop(2 * part, 2 * part + 2, step, 0)
+            norm_copy(i, part).start()
+
+    def norm_copy(i, part):
+        rows = nrm.at[i, s, pl.ds(64 * part, 64)]
+        return remote(rows, rows, ns.at[i, part], nr.at[i, part], sib)
 
     def branch_copy(i, half):
         part = pl.ds(3 * half, 3)
         return remote(bsend.at[i, part], brecv.at[i, part], bs.at[i, half], br.at[i, half], sib)
 
-    def wait_halo(i):
+    def wait_halo(i, h):
         @pl.when(r > 0)
         def _():
-            halo_down(i).wait_recv()
+            halo_down(i, h).wait_recv()
 
         @pl.when(r < 7)
         def _():
-            halo_up(i).wait_recv()
+            halo_up(i, h).wait_recv()
 
     def tile(n):
         return slice(256 * n, 256 * n + 256)
@@ -255,32 +263,71 @@
             for k in range(2):
                 acc[k, dx, rows, :] = acc[k, dx, rows, :] + h[128 * k : 128 * k + 128]
 
-        reg = lax.broadcasted_iota(jnp.int32, (REG, 192), 0)
+        out = None
         for k in range(2):
-            img = 2 * k + i
             total = shifted(acc[k, 0], 1, col192) + acc[k, 1] + shifted(acc[k, 2], -1, col192)
-            above = jnp.where(r > 0, rids[jnp.maximum(r - 1, 0), img, 3:4, :], -1)
-            below = jnp.where(r < 7, rids[jnp.minimum(r + 1, 7), img, 0:1, :], -1)
-            ids = jnp.concatenate(
-                [above] + [rids[r, img, y : y + 1, :] for y in range(4)] + [below], axis=1
-            )
-            onehot = jnp.where(reg == ids, 1.0, 0.0).astype(BF16)
-            hi, mid, lo = split3(total)
-            pooled[64 * img : 64 * img + 64, :] = dot(onehot, hi) + dot(onehot, mid) + dot(onehot, lo)
+            total = jnp.concatenate([total, jnp.zeros((64, 256), F32)], axis=0)
+            for part in split3(total):
+                term = dot(spot[2 * k + i], part)
+                out = term if out is None else out + term
+        if i == 0:
+            ordered[...] = out.reshape(8, 32, 256)
+        else:
+            ordered[...] = ordered[...] + out.reshape(8, 32, 256)
+
+    wait_halo(0, 0)
+    halo_part(0, 0)
+    halo_sent(0, 0)
+    halo_sent(0, 1)
+    for copy in rid_copies:
+        copy.start()
+    start_halo(1, 0)
+    loads["gain"].wait()
+    loads["scale"].wait()
+    wait_halo(0, 1)
+    halo_part(0, 1)
+    start_halo(1, 1)
+    for copy in key_rows:
+        copy.start()
+    layer_norm(0)
+    loads["w1"].wait()
+    loads["w2"].wait()
+
+    for part in range(2):
+        norm_copy(0, part).wait()
+    mlp(0)
 
     for copy in rid_copies:
         copy.wait()
-    loads["rid"].wait()
-    loads["gain"].wait()
-    loads["scale"].wait()
-
-    wait_halo(0)
-    halo_part(0)
-    layer_norm(0)
-    norm_copy(0).start()
-    loads["w1"].wait()
-    loads["w2"].wait()
-
+    for name in ("rid", "own", "par"):
+        loads[name].wait()
+    place = lax.broadcasted_iota(jnp.int32, (256, REG), 0)
+    reg = lax.broadcasted_iota(jnp.int32, (REG, 256), 0)
+    for img in range(4):
+        above = jnp.where(r > 0, rids[jnp.maximum(r - 1, 0), img, 3:4, :], -1)
+        below = jnp.where(r < 7, rids[jnp.minimum(r + 1, 7), img, 0:1, :], -1)
+        rest = jnp.full((1, 64), -1, jnp.int32)
+        ids = jnp.concatenate(
+            [above] + [rids[r, img, y : y + 1, :] for y in range(4)] + [below, rest], axis=1
+        )
+        onehot = jnp.where(reg == ids, 1.0, 0.0).astype(BF16)
+        perm = jnp.where(place == ownv[:, REG * img : REG * img + REG], 1.0, 0.0).astype(BF16)
+        spot[img] = dot(perm, onehot).astype(BF16)
+
+    wait_halo(1, 0)
+    halo_part(1, 0)
+    wait_halo(1, 1)
+    halo_part(1, 1)
+    layer_norm(1)
+    halo_sent(1, 0)
+    halo_sent(1, 1)
+    loads["pe"].wait()
+    loads["pk"].wait()
+    merge(0)
+    expand(0)
+    for part in range(2):
+        norm_copy(1, part).wait()
+    mlp(1)
     for copy in key_rows:
         copy.wait()
     loads["key"].wait()
@@ -290,45 +337,28 @@
     ]
     for copy in key_batch:
         copy.start()
-
-    norm_copy(0).wait()
-    mlp(0)
-
-    wait_halo(1)
-    halo_sent(1)
-    halo_part(1)
-    layer_norm(1)
-    norm_copy(1).start()
-    loads["pe"].wait()
-    loads["pk"].wait()
-    merge(0)
-    expand(0)
-    norm_copy(1).wait()
-    mlp(1)
     project(0)
+    merge(1)
+    expand(1)
+    project(1)
+
+    ordered16[...] = ordered[...].astype(BF16)
+    pool_copies = []
+    for d in (2, 6, 3, 5, 1, 7, 4):
+        block = ordered16.at[lax.rem(r + d, 8)]
+        pool_copies.append(remote(block, gathered.at[0, d], ps.at[0, d], pr.at[0, d], row_peer[d - 1]))
+        pool_copies.append(remote(block, gathered.at[1, d], ps.at[1, d], pr.at[1, d], cross_peer[d - 1]))
+    pool_copies.append(remote(ordered16.at[r], gathered.at[1, 0], ps.at[1, 0], pr.at[1, 0], sib))
+    for copy in pool_copies:
+        copy.start()
+
     for copy in key_batch:
         copy.wait()
     key_sib = []
     for d in range(1, 8):
         part = pl.ds(lax.rem(b + 8 - d, 8) * 8 + 4 * s, 4)
         key_sib.append(remote(kall.at[part], kall.at[part], ks3.at[d], kr3.at[d], sib))
-    merge(1)
     for copy in key_sib:
-        copy.start()
-    expand(1)
-    project(1)
-
-    loads["own"].wait()
-    loads["par"].wait()
-    place = lax.broadcasted_iota(jnp.int32, (256, 256), 0)
-    perm = jnp.where(place == ownv[...], 1.0, 0.0).astype(BF16)
-    hi, mid, lo = split3(pooled[...])
-    ordered[...] = (dot(perm, hi) + dot(perm, mid) + dot(perm, lo)).reshape(8, 32, 256)
-    pool_copies = [
-        remote(ordered.at[lax.rem(r + d, 8)], gathered.at[d], ps.at[d], pr.at[d], row_peer[d - 1])
-        for d in range(1, 8)
-    ]
-    for copy in pool_copies:
         copy.start()
 
     for copy in key_sib:
@@ -362,14 +392,12 @@
 
     for copy in pool_copies:
         copy.wait()
-    total = ordered[r]
+    same = ordered16[r].astype(F32)
+    cross = gathered[1, 0].astype(F32)
     for d in range(1, 8):
-        total = total + gathered[d]
-    sibsum[0] = total
-    sib_copy = remote(sibsum.at[0], sibsum.at[1], ss.at[0], sr.at[0], sib)
-    sib_copy.start()
-    sib_copy.wait()
-    total = sibsum[0] + sibsum[1]
+        same = same + gathered[0, d].astype(F32)
+        cross = cross + gathered[1, d].astype(F32)
+    total = same + cross
     probe = total * lax.rsqrt(jnp.sum(total * total, axis=1, keepdims=True) + NORM_EPS)
     emb_o[...] = probe
     hi, mid, lo = split3(probe)
@@ -414,23 +442,22 @@
         vmem((256, 1536), BF16),
         vmem((256, 1024), BF16),
         vmem((2, 3, 192, 256), F32),
-        vmem((256, 256), F32),
+        vmem((4, 256, 256), BF16),
         vmem((8, 32, 256), F32),
-        vmem((8, 32, 256), F32),
-        vmem((2, 32, 256), F32),
+        vmem((8, 32, 256), BF16),
+        vmem((2, 8, 32, 256), BF16),
         vmem((8, 4, 4, 32), jnp.int32),
         vmem((64, 32, 256), BF16),
         vmem((8, 2048), F32),
         dma((12,)),
+        dma((2, 2, 2)), dma((2, 2, 2)),
         dma((2, 2)), dma((2, 2)),
-        dma((2,)), dma((2,)),
         dma((2, 2)), dma((2, 2)),
         dma((8,)), dma((8,)),
         dma((8,)), dma((8,)),
         dma((8,)), dma((8,)),
         dma((8,)), dma((8,)),
-        dma((8,)), dma((8,)),
-        dma((1,)), dma((1,)),
+        dma((2, 8)), dma((2, 8)),
     ]
     emb, loss = pl.pallas_call(
         kernel,

time: 50.6 us -> 48.7 us (0.962)
  Pallas kernels: 49.8 us -> 47.7 us
    pallas_call x1, Pallas kernels: 48.4 us -> 46.3 us  [body(): pl.pallas_call(kernel, out_shape=(jax.ShapeDtypeStruct((32, 256), F32), j...]
where the time goes in v3:
time: 48.7 us; the launch traced here: 48.3 us
  Pallas kernels  47.7 us (98%)
  between operations  0.64 us (1%)
    pallas_call x1, Pallas kernels, body(): pl.pallas_call(kernel, out_shape=(jax.ShapeDtypeStruct((32, 256), F32), j...  46.3 us
    pallas_call x1, Pallas kernels, body(): pl.pallas_call(finish, out_shape=(jax.ShapeDtypeStruct((32, 256), F32), j...  1.38 us

profile of v3, /device:TPU:1, one launch (start us, length us, event | category | flops | bytes accessed | tf_op | source)
XLA Modules:
  0.0 48.3 jit_solution(11053489626345160200)
XLA Ops:
  0.6 46.3 %region_loss.1 = (f32[32,256]{1,0:T(8,128)}, f32[1,32]{1,0:T(1,128)}) custom-call(bf16[4,4,32,1536]{3,2,1,0:T(8,128)(2,1)} %f.1, bf16[7,7,1536]{2,1,0:T(8,128)(2,1)} %dwk.1, bf16[1536]{0:T(1024)(128)(2,1)} %gain.1, bf16[1536,1536]{1,0:T(8,128)(2,1)} %w1.1, bf16[1536,1536]{1,0:T(8,128)(2,1)} %w2.1, bf16[1536]{0:T(1024)(128)(2,1)} %scale.1, ...), custom_call_target="tpu_custom_call" | custom-call | tf_op jit(solution)/shard_map/region_loss/pallas_call | solution.py:462
  46.9 1.4 %finish.1 = (f32[32,256]{1,0:T(8,128)}, f32[1,32]{1,0:T(1,128)}) custom-call(f32[32,256]{1,0:T(8,128)} %get-tuple-element.6.emb, f32[1,32]{1,0:T(1,128)} %get-tuple-element.7.loss), custom_call_target="tpu_custom_call" | custom-call | tf_op jit(solution)/shard_map/finish/pallas_call | solution.py:476

commit v4 on v3

--- a/solution.py
+++ b/solution.py
@@ -48,7 +48,7 @@
     fv, halo, dwv, dwf, w1v, w2v, pev, pkv, gv, sv, ownv, parv,
     taps, nrm, inner, bpart, bsend, brecv, bo, hid, acc, spot, ordered, ordered16, gathered,
     rids, kall, knorm,
-    lsem, hs, hr, ns, nr, bs, br, rs1, rr1, ks1, kr1, ks2, kr2, ks3, kr3, ps, pr,
+    lsem, hs, hr, ns, nr, bs, br, rs1, rr1, ks1, kr1, ks2, kr2, kzs, kzr, ks3, kr3, ps, pr,
 ):
     b = lax.axis_index("batch")
     r = lax.axis_index("rows")
@@ -58,11 +58,22 @@
     down = (b, jnp.minimum(r + 1, 7), s)
     row_peer = [(b, lax.rem(r + d, 8), s) for d in range(1, 8)]
     cross_peer = [(b, lax.rem(r + d, 8), 1 - s) for d in range(1, 8)]
-    batch_peer = [(lax.rem(b + d, 8), r, s) for d in range(1, 8)]
+    z = b // 2
+    beside = (b + 1 - 2 * (b % 2), r, s)
+    above_z = (jnp.minimum(b + 2, 6 + b % 2), r, s)
+    below_z = (jnp.maximum(b - 2, b % 2), r, s)
 
     barrier = pltpu.get_barrier_semaphore()
-    for device in [sib] + row_peer + cross_peer + batch_peer:
+    for device in [sib, beside] + row_peer + cross_peer:
         pl.semaphore_signal(barrier, inc=1, device_id=device, device_id_type=MESH)
+
+    @pl.when(z < 3)
+    def _():
+        pl.semaphore_signal(barrier, inc=1, device_id=above_z, device_id_type=MESH)
+
+    @pl.when(z > 0)
+    def _():
+        pl.semaphore_signal(barrier, inc=1, device_id=below_z, device_id_type=MESH)
 
     def local(src, dst, i):
         return pltpu.make_async_copy(src, dst, lsem.at[i])
@@ -76,7 +87,7 @@
         "f": local(f, fv, 0),
         "dw": local(dwk, dwv, 1),
         "rid": local(rid, rids.at[r], 2),
-        "key": local(key, kall.at[b * 8 + r], 3),
+        "key": local(key.at[pl.ds(16 * s, 16)], kall.at[s, b * 8 + r], 3),
         "own": local(own, ownv, 4),
         "par": local(par, parv, 5),
         "w1": local(w1, w1v, 6),
@@ -89,7 +100,8 @@
     for name in ("dw", "f", "gain", "scale", "rid", "key", "own", "par", "w1", "w2", "pe", "pk"):
         loads[name].start()
 
-    pl.semaphore_wait(barrier, 22)
+    pl.semaphore_wait(barrier, 17 + z * (3 - z) // 2)
+
 
     def halo_up(i, h):
         lanes = pl.ds(768 * h, 768)
@@ -128,8 +140,49 @@
         remote(rid, rids.at[r], rs1.at[d], rr1.at[d], row_peer[d]) for d in range(7)
     ]
     key_rows = [
-        remote(key, kall.at[b * 8 + r], ks1.at[d], kr1.at[d], row_peer[d]) for d in range(7)
+        remote(key.at[pl.ds(16 * s, 16)], kall.at[s, b * 8 + r], ks1.at[d], kr1.at[d], row_peer[d])
+        for d in range(7)
     ]
+    for copy in key_rows:
+        copy.start()
+
+    eight = kall.at[s, pl.ds(b * 8, 8)]
+    key_beside = remote(eight, eight, ks2.at[0], kr2.at[0], beside)
+
+    def key_up(k):
+        plane = kall.at[s, pl.ds(jnp.maximum(z - k, 0) * 16, 16)]
+        return remote(plane, plane, kzs.at[0, k], kzr.at[0, k], above_z)
+
+    def key_down(k):
+        plane = kall.at[s, pl.ds(jnp.minimum(z + k, 3) * 16, 16)]
+        return remote(plane, plane, kzs.at[1, k], kzr.at[1, k], below_z)
+
+    def start_keys(k):
+        @pl.when((z < 3) & (z >= k))
+        def _():
+            key_up(k).start()
+
+        @pl.when((z > 0) & (z + k <= 3))
+        def _():
+            key_down(k).start()
+
+    def wait_keys(k):
+        @pl.when((z < 3) & (z >= k))
+        def _():
+            key_up(k).wait_send()
+
+        @pl.when((z > 0) & (z + k <= 3))
+        def _():
+            key_down(k).wait_send()
+
+        @pl.when(z >= k + 1)
+        def _():
+            key_up(k).wait_recv()
+
+        @pl.when(z + k + 1 <= 3)
+        def _():
+            key_down(k).wait_recv()
+
     for i in range(2):
         @pl.when(r == 0)
         def _():
@@ -277,6 +330,10 @@
 
     wait_halo(0, 0)
     halo_part(0, 0)
+    for copy in key_rows:
+        copy.wait()
+    loads["key"].wait()
+    key_beside.start()
     halo_sent(0, 0)
     halo_sent(0, 1)
     for copy in rid_copies:
@@ -287,14 +344,14 @@
     wait_halo(0, 1)
     halo_part(0, 1)
     start_halo(1, 1)
-    for copy in key_rows:
-        copy.start()
     layer_norm(0)
     loads["w1"].wait()
     loads["w2"].wait()
 
     for part in range(2):
         norm_copy(0, part).wait()
+    key_beside.wait()
+    start_keys(0)
     mlp(0)
 
     for copy in rid_copies:
@@ -319,6 +376,8 @@
     wait_halo(1, 1)
     halo_part(1, 1)
     layer_norm(1)
+    wait_keys(0)
+    start_keys(1)
     halo_sent(1, 0)
     halo_sent(1, 1)
     loads["pe"].wait()
@@ -328,16 +387,9 @@
     for part in range(2):
         norm_copy(1, part).wait()
     mlp(1)
-    for copy in key_rows:
-        copy.wait()
-    loads["key"].wait()
-    half = pl.ds(b * 8 + 4 * s, 4)
-    key_batch = [
-        remote(kall.at[half], kall.at[half], ks2.at[d], kr2.at[d], batch_peer[d]) for d in range(7)
-    ]
-    for copy in key_batch:
-        copy.start()
     project(0)
+    wait_keys(1)
+    start_keys(2)
     merge(1)
     expand(1)
     project(1)
@@ -352,22 +404,15 @@
     for copy in pool_copies:
         copy.start()
 
-    for copy in key_batch:
-        copy.wait()
-    key_sib = []
-    for d in range(1, 8):
-        part = pl.ds(lax.rem(b + 8 - d, 8) * 8 + 4 * s, 4)
-        key_sib.append(remote(kall.at[part], kall.at[part], ks3.at[d], kr3.at[d], sib))
-    for copy in key_sib:
-        copy.start()
-
-    for copy in key_sib:
-        copy.wait()
+    key_sib = remote(kall.at[s], kall.at[s], ks3.at[0], kr3.at[0], sib)
+    wait_keys(2)
+    key_sib.start()
+    key_sib.wait()
 
     ones = jnp.ones((8, 256), BF16)
 
     def key_norms(n, _):
-        k = kall[pl.ds(n * 8, 8)].reshape(256, 256).astype(F32)
+        k = kall[n // 4, pl.ds(n % 4 * 16, 16)].reshape(256, 256).astype(F32)
         sq = k * k
         top = sq.astype(BF16)
         bottom = (sq - top.astype(F32)).astype(BF16)
@@ -379,7 +424,8 @@
 
     slot = lax.broadcasted_iota(jnp.int32, (1, 256), 1)
     partner = jnp.concatenate([parv[k : k + 1, :] for k in range(4)], axis=1)
-    positive = (slot // REG * REG + b * 256 + partner).astype(F32)
+    target = slot // REG * REG + b * 256 + partner
+    positive = (target // 16 % 2 * 1024 + target // 32 * 16 + target % 16).astype(F32)
     used = jnp.zeros((1, 256), F32)
     for k in range(4):
         ids = jnp.max(rids[:, k].astype(F32), axis=0)
@@ -447,7 +493,7 @@
         vmem((8, 32, 256), BF16),
         vmem((2, 8, 32, 256), BF16),
         vmem((8, 4, 4, 32), jnp.int32),
-        vmem((64, 32, 256), BF16),
+        vmem((2, 64, 16, 256), BF16),
         vmem((8, 2048), F32),
         dma((12,)),
         dma((2, 2, 2)), dma((2, 2, 2)),
@@ -455,8 +501,9 @@
         dma((2, 2)), dma((2, 2)),
         dma((8,)), dma((8,)),
         dma((8,)), dma((8,)),
-        dma((8,)), dma((8,)),
-        dma((8,)), dma((8,)),
+        dma((1,)), dma((1,)),
+        dma((2, 3)), dma((2, 3)),
+        dma((1,)), dma((1,)),
         dma((2, 8)), dma((2, 8)),
     ]
     emb, loss = pl.pallas_call(

time: 48.7 us -> 47.7 us (0.979)
  Pallas kernels: 47.7 us -> 46.9 us
    pallas_call x1, Pallas kernels: 46.3 us -> 45.5 us  [body(): pl.pallas_call(kernel, out_shape=(jax.ShapeDtypeStruct((32, 256), F32), j...]
where the time goes in v4:
time: 47.7 us; the launch traced here: 47.5 us
  Pallas kernels  46.9 us (98%)
  between operations  0.64 us (1%)
    pallas_call x1, Pallas kernels, body(): pl.pallas_call(kernel, out_shape=(jax.ShapeDtypeStruct((32, 256), F32), j...  45.5 us
    pallas_call x1, Pallas kernels, body(): pl.pallas_call(finish, out_shape=(jax.ShapeDtypeStruct((32, 256), F32), j...  1.38 us

profile of v4, /device:TPU:1, one launch (start us, length us, event | category | flops | bytes accessed | tf_op | source)
XLA Modules:
  0.0 47.5 jit_solution(17135587986191114327)
XLA Ops:
  0.6 45.5 %region_loss.1 = (f32[32,256]{1,0:T(8,128)}, f32[1,32]{1,0:T(1,128)}) custom-call(bf16[4,4,32,1536]{3,2,1,0:T(8,128)(2,1)} %f.1, bf16[7,7,1536]{2,1,0:T(8,128)(2,1)} %dwk.1, bf16[1536]{0:T(1024)(128)(2,1)} %gain.1, bf16[1536,1536]{1,0:T(8,128)(2,1)} %w1.1, bf16[1536,1536]{1,0:T(8,128)(2,1)} %w2.1, bf16[1536]{0:T(1024)(128)(2,1)} %scale.1, ...), custom_call_target="tpu_custom_call" | custom-call | tf_op jit(solution)/shard_map/region_loss/pallas_call | solution.py:509
  46.2 1.4 %finish.1 = (f32[32,256]{1,0:T(8,128)}, f32[1,32]{1,0:T(1,128)}) custom-call(f32[32,256]{1,0:T(8,128)} %get-tuple-element.6.emb, f32[1,32]{1,0:T(1,128)} %get-tuple-element.7.loss), custom_call_target="tpu_custom_call" | custom-call | tf_op jit(solution)/shard_map/finish/pallas_call | solution.py:523

commit v5 on v4

--- a/solution.py
+++ b/solution.py
@@ -407,7 +407,6 @@
     key_sib = remote(kall.at[s], kall.at[s], ks3.at[0], kr3.at[0], sib)
     wait_keys(2)
     key_sib.start()
-    key_sib.wait()
 
     ones = jnp.ones((8, 256), BF16)
 
@@ -420,7 +419,9 @@
         knorm[:, pl.ds(pl.multiple_of(n * 256, 256), 256)] = lax.rsqrt(total + NORM_EPS) * 10.0
         return 0
 
-    lax.fori_loop(0, 8, key_norms, 0)
+    lax.fori_loop(4 * s, 4 * s + 4, key_norms, 0)
+    key_sib.wait()
+    lax.fori_loop(4 - 4 * s, 8 - 4 * s, key_norms, 0)
 
     slot = lax.broadcasted_iota(jnp.int32, (1, 256), 1)
     partner = jnp.concatenate([parv[k : k + 1, :] for k in range(4)], axis=1)

time: 47.7 us -> 47.7 us (level)
  no operation moved by 1% of the time
where the time goes in v5:
time: 47.7 us; the launch traced here: 47.5 us
  Pallas kernels  46.9 us (98%)
  between operations  0.64 us (1%)
    pallas_call x1, Pallas kernels, body(): pl.pallas_call(kernel, out_shape=(jax.ShapeDtypeStruct((32, 256), F32), j...  45.5 us
    pallas_call x1, Pallas kernels, body(): pl.pallas_call(finish, out_shape=(jax.ShapeDtypeStruct((32, 256), F32), j...  1.38 us

profile of v5, /device:TPU:1, one launch (start us, length us, event | category | flops | bytes accessed | tf_op | source)
XLA Modules:
  0.0 47.5 jit_solution(7932510649714702890)
XLA Ops:
  0.6 45.5 %region_loss.1 = (f32[32,256]{1,0:T(8,128)}, f32[1,32]{1,0:T(1,128)}) custom-call(bf16[4,4,32,1536]{3,2,1,0:T(8,128)(2,1)} %f.1, bf16[7,7,1536]{2,1,0:T(8,128)(2,1)} %dwk.1, bf16[1536]{0:T(1024)(128)(2,1)} %gain.1, bf16[1536,1536]{1,0:T(8,128)(2,1)} %w1.1, bf16[1536,1536]{1,0:T(8,128)(2,1)} %w2.1, bf16[1536]{0:T(1024)(128)(2,1)} %scale.1, ...), custom_call_target="tpu_custom_call" | custom-call | tf_op jit(solution)/shard_map/region_loss/pallas_call | solution.py:510
  46.2 1.4 %finish.1 = (f32[32,256]{1,0:T(8,128)}, f32[1,32]{1,0:T(1,128)}) custom-call(f32[32,256]{1,0:T(8,128)} %get-tuple-element.6.emb, f32[1,32]{1,0:T(1,128)} %get-tuple-element.7.loss), custom_call_target="tpu_custom_call" | custom-call | tf_op jit(solution)/shard_map/finish/pallas_call | solution.py:524
